TPU v7x, 256 devices: a whole 4x4x8 slice. The times are simulated.
256 devices in a mesh: seq: 32 (over z, x_lo, core), chan: 8 (over x_hi, y).
Axes of the slice: x: 4 (x_hi: 2, x_lo: 2; x = x_hi * 2 + x_lo), y: 4, z: 8, core: 2. Of those that a mesh axis runs over, the one named last changes fastest.
Arguments:
- q_gate: float32 [16384, 2048], P('seq', 'chan'), may hold values from -6 to 6
- k_gate: float32 [16384, 2048], P('seq', 'chan'), may hold values from -6 to 6
- values: float32 [16384, 2048], P('seq', 'chan'), may hold values from -6 to 6
- filter_raw: float32 [16384, 128], P('seq'), may hold values from -6 to 6
- grad_out: float32 [16384, 2048], P('seq', 'chan'), may hold values from -6 to 6
Outputs:
- grad_q: float32 [16384, 2048], P('seq', 'chan')
- grad_k: float32 [16384, 2048], P('seq', 'chan')
- grad_v: float32 [16384, 2048], P('seq', 'chan')
- grad_filter: float32 [16384, 128], P('seq')
All inputs are finite; a program needn't handle non-finite values.
Results may differ from a plain program's by a relative error of at most 0.0001.
Values sent between devices are 32-bit elements; how exact they have to be, the bound alone decides.
No kernel may reach another device: no remote copies, remote signals or barrier semaphores. Data moves between devices by JAX's collectives and lax.ppermute only.
A program may use at most 64 MiB of HBM per device.

v0:
```python
import math
import jax
import jax.numpy as jnp
from jax import lax
from jax.sharding import PartitionSpec as P


def product_hi(form, left, right):
    return jnp.einsum(form, left, right, precision=lax.Precision.HIGHEST)


def angle_table(first, second, modulus):
    counts = first[:, None] * second[None, :] % modulus
    angles = counts.astype(jnp.float32) * (2.0 * math.pi / modulus)
    return (jnp.cos(angles), jnp.sin(angles))


def forward_transform(block, shards, offset_base, cos_coarse, sin_coarse, cos_fine, sin_fine):
    seq_len = block.shape[0]
    coarse = 2 * shards
    total = coarse * seq_len
    share = seq_len // shards
    spread = lax.all_to_all(block[None], "seq", split_axis=1, concat_axis=0, tiled=True)
    real_part = product_hi("kn,nbw->kbw", cos_coarse, spread)
    imag_part = -product_hi("kn,nbw->kbw", sin_coarse, spread)
    offsets = offset_base * share + jnp.arange(share, dtype=jnp.int32)
    freq_rows = jnp.arange(coarse, dtype=jnp.int32)
    twist_cos, twist_sin = angle_table(freq_rows, offsets, total)
    twist_cos = twist_cos[:, :, None]
    twist_sin = twist_sin[:, :, None]
    turned_real = real_part * twist_cos + imag_part * twist_sin
    turned_imag = imag_part * twist_cos - real_part * twist_sin
    moved_real, moved_imag = (
        lax.all_to_all(turned_real, "seq", split_axis=0, concat_axis=1, tiled=True),
        lax.all_to_all(turned_imag, "seq", split_axis=0, concat_axis=1, tiled=True),
    )
    spec_real = product_hi("kn,tnw->tkw", cos_fine, moved_real) + product_hi(
        "kn,tnw->tkw", sin_fine, moved_imag
    )
    spec_imag = product_hi("kn,tnw->tkw", cos_fine, moved_imag) - product_hi(
        "kn,tnw->tkw", sin_fine, moved_real
    )
    return (spec_real, spec_imag)


def inverse_transform(spec_real, spec_imag, shards, offset_base, cos_fine, sin_fine):
    seq_len = spec_real.shape[1]
    coarse = 2 * shards
    total = coarse * seq_len
    part_real = product_hi("nk,tkw->tnw", cos_fine, spec_real) - product_hi(
        "nk,tkw->tnw", sin_fine, spec_imag
    )
    part_imag = product_hi("nk,tkw->tnw", cos_fine, spec_imag) + product_hi(
        "nk,tkw->tnw", sin_fine, spec_real
    )
    local_freq = 2 * offset_base + jnp.arange(2, dtype=jnp.int32)
    positions = jnp.arange(seq_len, dtype=jnp.int32)
    twist_cos, twist_sin = angle_table(local_freq, positions, total)
    twist_cos = twist_cos[:, :, None]
    twist_sin = twist_sin[:, :, None]
    turned_real = part_real * twist_cos - part_imag * twist_sin
    turned_imag = part_imag * twist_cos + part_real * twist_sin
    moved_real, moved_imag = (
        lax.all_to_all(turned_real, "seq", split_axis=1, concat_axis=0, tiled=True),
        lax.all_to_all(turned_imag, "seq", split_axis=1, concat_axis=0, tiled=True),
    )
    rows_out = jnp.arange(shards, dtype=jnp.int32)
    freq_rows = jnp.arange(coarse, dtype=jnp.int32)
    back_cos, back_sin = angle_table(rows_out, freq_rows, coarse)
    spatial = (
        product_hi("nk,kbw->nbw", back_cos, moved_real)
        - product_hi("nk,kbw->nbw", back_sin, moved_imag)
    ) * (1.0 / total)
    placed = lax.all_to_all(spatial, "seq", split_axis=0, concat_axis=1, tiled=True)
    return placed[0]


def local(q_gate, k_gate, values, filter_raw, grad_out):
    seq_len = q_gate.shape[0]
    width = q_gate.shape[1]
    nfilt = filter_raw.shape[1]
    shards = lax.axis_size("seq")
    offset_base = lax.axis_index("seq")
    scale = float(seq_len * shards) ** (-0.5)
    coarse_rows = jnp.arange(2 * shards, dtype=jnp.int32)
    cos_coarse, sin_coarse = angle_table(
        coarse_rows, jnp.arange(shards, dtype=jnp.int32), 2 * shards
    )
    fine_rows = jnp.arange(seq_len, dtype=jnp.int32)
    cos_fine, sin_fine = angle_table(fine_rows, fine_rows, seq_len)
    gated = k_gate * values
    grad_conv = grad_out * q_gate
    filt = filter_raw * scale

    def forward(block):
        return forward_transform(
            block, shards, offset_base, cos_coarse, sin_coarse, cos_fine, sin_fine
        )

    def inverse(real_part, imag_part):
        return inverse_transform(real_part, imag_part, shards, offset_base, cos_fine, sin_fine)

    gated_real, gated_imag = forward(gated)
    grad_real, grad_imag = forward(grad_conv)
    filt_real, filt_imag = forward(filt)
    repeats = width // nfilt
    wide_real = jnp.tile(filt_real, (1, 1, repeats))
    wide_imag = jnp.tile(filt_imag, (1, 1, repeats))
    conv_real = wide_real * gated_real - wide_imag * gated_imag
    conv_imag = wide_real * gated_imag + wide_imag * gated_real
    back_real = wide_real * grad_real + wide_imag * grad_imag
    back_imag = wide_real * grad_imag - wide_imag * grad_real
    corr_real = gated_real * grad_real + gated_imag * grad_imag
    corr_imag = gated_real * grad_imag - gated_imag * grad_real
    folded_real = jnp.sum(corr_real.reshape(2, seq_len, repeats, nfilt), axis=2)
    folded_imag = jnp.sum(corr_imag.reshape(2, seq_len, repeats, nfilt), axis=2)
    filter_real, filter_imag = (folded_real, folded_imag)
    conv = inverse(conv_real, conv_imag)
    grad_gated = inverse(back_real, back_imag)
    corr = inverse(filter_real, filter_imag)
    grad_filter = lax.psum(corr, "chan") * scale
    grad_q = grad_out * conv
    grad_k = grad_gated * values
    grad_v = grad_gated * k_gate
    return (grad_q, grad_k, grad_v, grad_filter)


def solution(mesh):
    placed = (
        P("seq", "chan"),
        P("seq", "chan"),
        P("seq", "chan"),
        P("seq", None),
        P("seq", "chan"),
    )
    return jax.shard_map(
        local,
        mesh=mesh,
        in_specs=placed,
        out_specs=(P("seq", "chan"), P("seq", "chan"), P("seq", "chan"), P("seq", None)),
        check_vma=False,
    )
```

profile of v0, /device:TPU:32, one launch (start us, length us, event | category | flops | bytes accessed | tf_op | source)
XLA Modules:
  0.0 699.3 jit_solution(10144373009887755012)
XLA Ops:
  7.2 1.8 broadcast_multiply_fusion.1
  8.9 9.7 %all-to-all-start = ((f32[1,512,128]{2,0,1:T(1,128)}), f32[1,512,128]{2,0,1:T(1,128)S(1)}, u32[]{:S(2)}, u32[]{:S(2)}) async-start(f32[1,512,128]{2,0,1:T(1,128)} %bitcast.3), calls=%async_computation | async-start | bytes 524288 | tf_op jit(solution)/shard_map/all_to_all | solution.py:23
  19.9 10.2 %all-to-all-done = f32[1,512,128]{2,0,1:T(1,128)S(1)} async-done(((f32[1,512,128]{2,0,1:T(1,128)}), f32[1,512,128]{2,0,1:T(1,128)S(1)}, u32[]{:S(2)}, u32[]{:S(2)}) %all-to-all-start) | async-done | bytes 262176 | tf_op jit(solution)/shard_map/all_to_all | solution.py:23
  30.0 4.7 all-to-all-start.3
  36.1 15.6 %all-to-all-done.3 = f32[1,512,256]{2,0,1:T(1,128)S(1)} async-done(((f32[1,512,256]{2,0,1:T(1,128)}), f32[1,512,256]{2,0,1:T(1,128)S(1)}, u32[]{:S(2)}, u32[]{:S(2)}) %all-to-all-start.3) | async-done | bytes 524320 | tf_op jit(solution)/shard_map/all_to_all | solution.py:23
  51.7 5.0 all-to-all-start.9
  59.5 14.1 %all-to-all-done.9 = f32[1,512,256]{2,0,1:T(1,128)S(1)} async-done(((f32[1,512,256]{2,0,1:T(1,128)}), f32[1,512,256]{2,0,1:T(1,128)S(1)}, u32[]{:S(2)}, u32[]{:S(2)}) %all-to-all-start.9) | async-done | bytes 524320 | tf_op jit(solution)/shard_map/all_to_all | solution.py:23
  73.6 5.0 all-to-all-start.2
  79.7 15.7 %all-to-all-done.2 = f32[64,16,128]{2,1,0:T(8,128)S(1)} async-done(((f32[64,16,128]{2,1,0:T(8,128)}), f32[64,16,128]{2,1,0:T(8,128)S(1)}, u32[]{:S(2)}, u32[]{:S(2)}) %all-to-all-start.2) | async-done | bytes 524320 | tf_op jit(solution)/shard_map/all_to_all | solution.py:35
  96.3 5.7 all-to-all-start.1
  105.9 1.7 multiply_add_fusion.1
  109.2 9.6 %all-to-all-done.1 = f32[64,16,128]{2,1,0:T(8,128)} async-done(((f32[64,16,128]{2,1,0:T(8,128)}), f32[64,16,128]{2,1,0:T(8,128)}, u32[]{:S(2)}, u32[]{:S(2)}) %all-to-all-start.1) | async-done | bytes 524320 | tf_op jit(solution)/shard_map/all_to_all | solution.py:34
  118.9 5.9 all-to-all-start.10
  126.3 26.6 %all-to-all-done.10 = f32[64,16,256]{2,1,0:T(8,128)} async-done(((f32[64,16,256]{2,1,0:T(8,128)}), f32[64,16,256]{2,1,0:T(8,128)}, u32[]{:S(2)}, u32[]{:S(2)}) %all-to-all-start.10) | async-done | bytes 1048608 | tf_op jit(solution)/shard_map/all_to_all | solution.py:34
  152.9 5.0 all-to-all-start.11
  159.5 26.5 %all-to-all-done.11 = f32[64,16,256]{2,1,0:T(8,128)S(1)} async-done(((f32[64,16,256]{2,1,0:T(8,128)}), f32[64,16,256]{2,1,0:T(8,128)S(1)}, u32[]{:S(2)}, u32[]{:S(2)}) %all-to-all-start.11) | async-done | bytes 1048608 | tf_op jit(solution)/shard_map/all_to_all | solution.py:35
  186.0 5.0 all-to-all-start.4
  192.9 26.3 %all-to-all-done.4 = f32[64,16,256]{2,1,0:T(8,128)S(1)} async-done(((f32[64,16,256]{2,1,0:T(8,128)}), f32[64,16,256]{2,1,0:T(8,128)S(1)}, u32[]{:S(2)}, u32[]{:S(2)}) %all-to-all-start.4) | async-done | bytes 1048608 | tf_op jit(solution)/shard_map/all_to_all | solution.py:34
  219.2 5.7 all-to-all-start.5
  224.9 5.8 fusion.46
  231.8 5.8 fusion.50
  237.6 6.4 fusion.4
  244.0 6.7 fusion.5
  252.2 7.5 %fusion.38 = f32[2,256,512]{2,1,0:T(8,128)S(1)} fusion(f32[2,512,256]{2,1,0:T(8,128)S(1)} %bitcast.255), kind=kOutput, calls=%fused_computation.67 | convolution fusion | flops 1614282752 | bytes 2097152 | tf_op jit(solution)/shard_map/kn,tnw->tkw/dot_general | solution.py:9
  259.7 8.0 %fusion.48 = f32[2,256,512]{2,1,0:T(8,128)} fusion(f32[2,512,256]{2,1,0:T(8,128)S(1)} %bitcast.238), kind=kOutput, calls=%fused_computation.77 | convolution fusion | flops 1614282752 | bytes 2097152 | tf_op jit(solution)/shard_map/kn,tnw->tkw/dot_general | solution.py:9
  267.7 8.0 %fusion.36 = f32[2,256,512]{2,1,0:T(8,128)} fusion(f32[2,512,256]{2,1,0:T(8,128)S(1)} %bitcast.257), kind=kOutput, calls=%fused_computation.65 | convolution fusion | flops 1614282752 | bytes 2097152 | tf_op jit(solution)/shard_map/kn,tnw->tkw/dot_general | solution.py:9
  275.7 8.2 %fusion.1 = f32[2,512,256]{1,2,0:T(8,128)} fusion(f32[2,256,512]{2,1,0:T(8,128)S(1)} %fusion.38, f32[2,512,256]{2,1,0:T(8,128)S(1)} %bitcast.258), kind=kOutput, calls=%fused_computation.18 | convolution fusion | flops 1614544896 | bytes 3145728 | tf_op jit(solution)/shard_map/kn,tnw->tkw/dot_general | solution.py:9
  285.2 7.5 %fusion.44 = f32[2,256,512]{2,1,0:T(8,128)S(1)} fusion(f32[2,512,256]{2,1,0:T(8,128)S(1)} %bitcast.259), kind=kOutput, calls=%fused_computation.73 | convolution fusion | flops 1614282752 | bytes 2097152 | tf_op jit(solution)/shard_map/kn,tnw->tkw/dot_general | solution.py:9
  292.7 7.6 %fusion.3 = f32[2,512,256]{1,2,0:T(8,128)S(1)} fusion(f32[2,256,512]{2,1,0:T(8,128)S(1)} %copy-done.28, f32[2,512,256]{2,1,0:T(8,128)S(1)} %bitcast.260), kind=kOutput, calls=%fused_computation.24 | convolution fusion | flops 1614544896 | bytes 3145728 | tf_op jit(solution)/shard_map/kn,tnw->tkw/dot_general | solution.py:9
  300.3 7.8 %fusion = f32[2,512,256]{1,2,0:T(8,128)S(1)} fusion(f32[2,256,512]{2,1,0:T(8,128)S(1)} %copy-done.26, f32[2,512,256]{2,1,0:T(8,128)S(1)} %bitcast.256), kind=kOutput, calls=%fused_computation.16 | convolution fusion | flops 1614544896 | bytes 3145728 | tf_op jit(solution)/shard_map/kn,tnw->tkw/dot_general | solution.py:9
  308.2 11.9 %multiply_add_fusion = (f32[2,512,256]{1,2,0:T(8,128)S(1)}, f32[2,512,256]{1,2,0:T(8,128)S(1)}, f32[2,512,256]{1,2,0:T(8,128)}, f32[2,512,256]{1,2,0:T(8,128)}, ...) fusion(f32[2,512,256]{1,2,0:T(8,128)S(1)} %fusion, f32[2,512,256]{1,2,0:T(8,128)S(1)} %fusion.3, ...), kind=kOutput, calls=%fused_computation.82 | convolution fusion | flops 1619263488 | bytes 12582912 | tf_op jit(solution)/shard_map/kn,tnw->tkw/dot_general | solution.py:9
  320.1 5.3 fusion.28
  325.6 5.7 fusion.30
  331.3 5.3 convolution_add_fusion.4
  336.7 5.4 add_bitcast_fusion.2
  343.1 8.8 %all-to-all-start.15 = ((f32[2,512,128]{2,0,1:T(2,128)}), f32[2,512,128]{2,0,1:T(2,128)S(1)}, u32[]{:S(2)}, u32[]{:S(2)}) async-start(f32[2,512,128]{2,0,1:T(2,128)} %copy.151), calls=%async_computation.15 | async-start | bytes 1048576 | tf_op jit(solution)/shard_map/all_to_all | solution.py:64
  352.9 6.3 fusion.32
  359.2 6.7 fusion.34
  365.9 6.7 convolution_add_fusion
  372.6 8.7 %all-to-all-start.16 = ((f32[2,512,128]{2,0,1:T(2,128)}), f32[2,512,128]{2,0,1:T(2,128)S(1)}, u32[]{:S(2)}, u32[]{:S(2)}) async-start(f32[2,512,128]{2,0,1:T(2,128)} %copy.154), calls=%async_computation.16 | async-start | bytes 1048576 | tf_op jit(solution)/shard_map/all_to_all | solution.py:65
  381.4 6.3 fusion.40
  387.7 6.7 convolution_subtract_fusion
  394.4 6.7 convolution_add_fusion.2
  403.8 8.8 %all-to-all-start.17 = ((f32[32,16,128]{2,1,0:T(8,128)}), f32[32,16,128]{2,1,0:T(8,128)S(1)}, u32[]{:S(2)}, u32[]{:S(2)}) async-start(f32[32,16,128]{2,1,0:T(8,128)} %copy.157), calls=%async_computation.17 | async-start | bytes 524288 | tf_op jit(solution)/shard_map/all_to_all | solution.py:74
  412.7 6.3 fusion.42
  419.0 7.3 %add_bitcast_fusion = (f32[2,512,256]{1,2,0:T(8,128)}, f32[2,512,256]{1,2,0:T(8,128)S(1)}, f32[2,512,256]{1,2,0:T(8,128)}, f32[2,512,256]{1,2,0:T(8,128)S(1)}) fusion(f32[2,256,512]{2,1,0:T(8,128)S(1)} %copy-done.21, f32[2,256,512]{2,1,0:T(8,128)S(1)} %copy-done.20, f32[2,512]{1,0:T(2,128)S(1)} %get-tuple-element.33, f32[2,512]{1,0:T(2,128)S(1)} %get-tuple-element.32, ...), kind=kOutput, calls=%fused_computation.83 | convolution fusion | flops 1617690624 | bytes 9445376 | tf_op jit(solution)/shard_map/nk,tkw->tnw/dot_general | solution.py:9
  428.3 8.3 %all-to-all-start.12 = ((f32[2,512,256]{2,0,1:T(2,128)}), f32[2,512,256]{2,0,1:T(2,128)S(1)}, u32[]{:S(2)}, u32[]{:S(2)}) async-start(f32[2,512,256]{2,0,1:T(2,128)} %copy.144), calls=%async_computation.12 | async-start | bytes 2097152 | tf_op jit(solution)/shard_map/all_to_all | solution.py:64
  437.9 26.7 %all-to-all-done.12 = f32[2,512,256]{2,0,1:T(2,128)S(1)} async-done(((f32[2,512,256]{2,0,1:T(2,128)}), f32[2,512,256]{2,0,1:T(2,128)S(1)}, u32[]{:S(2)}, u32[]{:S(2)}) %all-to-all-start.12) | async-done | bytes 1048608 | tf_op jit(solution)/shard_map/all_to_all | solution.py:64
  464.6 4.4 all-to-all-start.13
  469.0 2.3 copy.127
  471.3 25.8 %all-to-all-done.13 = f32[2,512,256]{2,0,1:T(2,128)S(1)} async-done(((f32[2,512,256]{2,0,1:T(2,128)}), f32[2,512,256]{2,0,1:T(2,128)S(1)}, u32[]{:S(2)}, u32[]{:S(2)}) %all-to-all-start.13) | async-done | bytes 1048608 | tf_op jit(solution)/shard_map/all_to_all | solution.py:65
  498.2 5.0 all-to-all-start.6
  504.5 26.8 %all-to-all-done.6 = f32[2,512,256]{2,0,1:T(2,128)S(1)} async-done(((f32[2,512,256]{2,0,1:T(2,128)}), f32[2,512,256]{2,0,1:T(2,128)S(1)}, u32[]{:S(2)}, u32[]{:S(2)}) %all-to-all-start.6) | async-done | bytes 1048608 | tf_op jit(solution)/shard_map/all_to_all | solution.py:64
  531.3 5.3 all-to-all-start.7
  536.7 1.8 copy.146
  538.5 3.0 all_to_all.246
  541.6 1.8 copy.149
  543.4 3.0 all_to_all.250
  549.4 15.2 %all-to-all-done.7 = f32[2,512,256]{2,0,1:T(2,128)S(1)} async-done(((f32[2,512,256]{2,0,1:T(2,128)}), f32[2,512,256]{2,0,1:T(2,128)S(1)}, u32[]{:S(2)}, u32[]{:S(2)}) %all-to-all-start.7) | async-done | bytes 1048608 | tf_op jit(solution)/shard_map/all_to_all | solution.py:65
  564.6 5.6 all-to-all-start.14
  576.0 11.2 %all-to-all-done.14 = f32[32,16,256]{2,1,0:T(8,128)} async-done(((f32[32,16,256]{2,1,0:T(8,128)}), f32[32,16,256]{2,1,0:T(8,128)}, u32[]{:S(2)}, u32[]{:S(2)}) %all-to-all-start.14) | async-done | bytes 524320 | tf_op jit(solution)/shard_map/all_to_all | solution.py:74
  587.2 5.1 all-to-all-start.8
  593.1 94.4 %all-reduce.2.cloned.1.call-done = f32[512,128]{1,0:T(8,128)} async-done(((f32[512,128]{1,0:T(8,128)}), f32[512,128]{1,0:T(8,128)}) %all-reduce.2.cloned.1.call-update) | async-done | bytes 262160 | tf_op jit(solution)/shard_map/psum | solution.py:121
  689.2 2.2 bitcast_multiply_fusion.8
  (122 shorter events, 44.3 us)
Async XLA Ops:
  7.2 11.4 %copy-start.6 = (f32[512,256]{1,0:T(8,128)S(1)}, f32[512,256]{1,0:T(8,128)}, u32[]{:S(2)}) copy-start(f32[512,256]{1,0:T(8,128)} %param.6) | copy-start | bytes 1572868
  7.2 11.4 %copy-start.8 = (f32[512,256]{1,0:T(8,128)S(1)}, f32[512,256]{1,0:T(8,128)}, u32[]{:S(2)}) copy-start(f32[512,256]{1,0:T(8,128)} %param.7) | copy-start | bytes 1572868
  8.9 21.1 %all-to-all-start = ((f32[1,512,128]{2,0,1:T(1,128)}), f32[1,512,128]{2,0,1:T(1,128)S(1)}, u32[]{:S(2)}, u32[]{:S(2)}) async-start(f32[1,512,128]{2,0,1:T(1,128)} %bitcast.3), calls=%async_computation | async-start | bytes 524288 | tf_op jit(solution)/shard_map/all_to_all | solution.py:23
  19.9 14.9 %copy-start.10 = (f32[512,256]{1,0:T(8,128)S(1)}, f32[512,256]{1,0:T(8,128)}, u32[]{:S(2)}) copy-start(f32[512,256]{1,0:T(8,128)} %param.9) | copy-start | bytes 1572868
  19.9 14.9 %copy-start.23 = (f32[512,256]{1,0:T(8,128)S(1)}, f32[512,256]{1,0:T(8,128)}, u32[]{:S(2)}) copy-start(f32[512,256]{1,0:T(8,128)} %param.5) | copy-start | bytes 1572868
  30.0 21.6 %all-to-all-start.3 = ((f32[1,512,256]{2,0,1:T(1,128)}), f32[1,512,256]{2,0,1:T(1,128)S(1)}, u32[]{:S(2)}, u32[]{:S(2)}) async-start(f32[1,512,256]{2,0,1:T(1,128)} %broadcast_in_dim.7), calls=%async_computation.3 | async-start | bytes 1048576 | tf_op jit(solution)/shard_map/all_to_all | solution.py:23
  51.7 21.9 %all-to-all-start.9 = ((f32[1,512,256]{2,0,1:T(1,128)}), f32[1,512,256]{2,0,1:T(1,128)S(1)}, u32[]{:S(2)}, u32[]{:S(2)}) async-start(f32[1,512,256]{2,0,1:T(1,128)} %broadcast_in_dim.8), calls=%async_computation.9 | async-start | bytes 1048576 | tf_op jit(solution)/shard_map/all_to_all | solution.py:23
  73.6 21.9 %all-to-all-start.2 = ((f32[64,16,128]{2,1,0:T(8,128)}), f32[64,16,128]{2,1,0:T(8,128)S(1)}, u32[]{:S(2)}, u32[]{:S(2)}) async-start(f32[64,16,128]{2,1,0:T(8,128)} %copy.112), calls=%async_computation.2 | async-start | bytes 1048576 | tf_op jit(solution)/shard_map/all_to_all | solution.py:35
  95.5 0.8 copy-start.12
  96.3 22.6 %all-to-all-start.1 = ((f32[64,16,128]{2,1,0:T(8,128)}), f32[64,16,128]{2,1,0:T(8,128)}, u32[]{:S(2)}, u32[]{:S(2)}) async-start(f32[64,16,128]{2,1,0:T(8,128)} %copy.109), calls=%async_computation.1 | async-start | bytes 1048576 | tf_op jit(solution)/shard_map/all_to_all | solution.py:34
  118.9 34.1 %all-to-all-start.10 = ((f32[64,16,256]{2,1,0:T(8,128)}), f32[64,16,256]{2,1,0:T(8,128)}, u32[]{:S(2)}, u32[]{:S(2)}) async-start(f32[64,16,256]{2,1,0:T(8,128)} %copy.136), calls=%async_computation.10 | async-start | bytes 2097152 | tf_op jit(solution)/shard_map/all_to_all | solution.py:34
  152.9 33.1 %all-to-all-start.11 = ((f32[64,16,256]{2,1,0:T(8,128)}), f32[64,16,256]{2,1,0:T(8,128)S(1)}, u32[]{:S(2)}, u32[]{:S(2)}) async-start(f32[64,16,256]{2,1,0:T(8,128)} %copy.139), calls=%async_computation.11 | async-start | bytes 2097152 | tf_op jit(solution)/shard_map/all_to_all | solution.py:35
  186.0 33.1 %all-to-all-start.4 = ((f32[64,16,256]{2,1,0:T(8,128)}), f32[64,16,256]{2,1,0:T(8,128)S(1)}, u32[]{:S(2)}, u32[]{:S(2)}) async-start(f32[64,16,256]{2,1,0:T(8,128)} %copy.117), calls=%async_computation.4 | async-start | bytes 2097152 | tf_op jit(solution)/shard_map/all_to_all | solution.py:34
  191.2 1.6 copy-start.13
  219.2 64.7 %all-to-all-start.5 = ((f32[64,16,256]{2,1,0:T(8,128)}), f32[64,16,256]{2,1,0:T(8,128)}, u32[]{:S(2)}, u32[]{:S(2)}) async-start(f32[64,16,256]{2,1,0:T(8,128)} %copy.120), calls=%async_computation.5 | async-start | bytes 2097152 | tf_op jit(solution)/shard_map/all_to_all | solution.py:35
  285.2 7.5 %copy-start.28 = (f32[2,256,512]{2,1,0:T(8,128)S(1)}, f32[2,256,512]{2,1,0:T(8,128)}, u32[]{:S(2)}) copy-start(f32[2,256,512]{2,1,0:T(8,128)} %fusion.48) | copy-start | bytes 3145732
  292.7 7.6 %copy-start.26 = (f32[2,256,512]{2,1,0:T(8,128)S(1)}, f32[2,256,512]{2,1,0:T(8,128)}, u32[]{:S(2)}) copy-start(f32[2,256,512]{2,1,0:T(8,128)} %fusion.36) | copy-start | bytes 3145732
  300.3 7.8 %copy-start.18 = (f32[2,512,256]{1,2,0:T(8,128)S(1)}, f32[2,512,256]{1,2,0:T(8,128)}, u32[]{:S(2)}) copy-start(f32[2,512,256]{1,2,0:T(8,128)} %fusion.1) | copy-start | bytes 3145732
  300.3 7.8 %copy-start.24 = (f32[2,512,128]{1,2,0:T(8,128)S(1)}, f32[2,512,128]{1,2,0:T(8,128)}, u32[]{:S(2)}) copy-start(f32[2,512,128]{1,2,0:T(8,128)} %fusion.4) | copy-start | bytes 1572868
  300.3 7.8 %copy-start.25 = (f32[2,512,128]{1,2,0:T(8,128)S(1)}, f32[2,512,128]{1,2,0:T(8,128)}, u32[]{:S(2)}) copy-start(f32[2,512,128]{1,2,0:T(8,128)} %fusion.5) | copy-start | bytes 1572868
  343.1 9.8 %copy-start.15 = (f32[2,512,256]{1,2,0:T(8,128)S(1)}, f32[2,512,256]{1,2,0:T(8,128)}, u32[]{:S(2)}) copy-start(f32[2,512,256]{1,2,0:T(8,128)} %get-tuple-element.18) | copy-start | bytes 3145732
  343.1 29.5 %all-to-all-start.15 = ((f32[2,512,128]{2,0,1:T(2,128)}), f32[2,512,128]{2,0,1:T(2,128)S(1)}, u32[]{:S(2)}, u32[]{:S(2)}) async-start(f32[2,512,128]{2,0,1:T(2,128)} %copy.151), calls=%async_computation.15 | async-start | bytes 1048576 | tf_op jit(solution)/shard_map/all_to_all | solution.py:64
  352.8 6.3 copy-start.17
  372.6 8.7 %copy-start.4 = (f32[2,512,256]{1,2,0:T(8,128)S(1)}, f32[2,512,256]{1,2,0:T(8,128)}, u32[]{:S(2)}) copy-start(f32[2,512,256]{1,2,0:T(8,128)} %get-tuple-element.20) | copy-start | bytes 3145732
  372.6 29.5 %all-to-all-start.16 = ((f32[2,512,128]{2,0,1:T(2,128)}), f32[2,512,128]{2,0,1:T(2,128)S(1)}, u32[]{:S(2)}, u32[]{:S(2)}) async-start(f32[2,512,128]{2,0,1:T(2,128)} %copy.154), calls=%async_computation.16 | async-start | bytes 1048576 | tf_op jit(solution)/shard_map/all_to_all | solution.py:65
  381.3 6.4 copy-start.16
  381.3 6.4 copy-start.27
  387.7 6.7 copy-start.14
  403.8 23.8 %all-to-all-start.17 = ((f32[32,16,128]{2,1,0:T(8,128)}), f32[32,16,128]{2,1,0:T(8,128)S(1)}, u32[]{:S(2)}, u32[]{:S(2)}) async-start(f32[32,16,128]{2,1,0:T(8,128)} %copy.157), calls=%async_computation.17 | async-start | bytes 524288 | tf_op jit(solution)/shard_map/all_to_all | solution.py:74
  412.6 6.4 copy-start.20
  412.6 6.4 copy-start.21
  412.7 6.4 copy-start.22
  427.6 9.0 %copy-start.5 = (f32[2,512,256]{1,2,0:T(8,128)S(1)}, f32[2,512,256]{1,2,0:T(8,128)}, u32[]{:S(2)}) copy-start(f32[2,512,256]{1,2,0:T(8,128)} %get-tuple-element.14) | copy-start | bytes 3145732
  427.6 0.7 copy-start.19
  428.3 36.3 %all-to-all-start.12 = ((f32[2,512,256]{2,0,1:T(2,128)}), f32[2,512,256]{2,0,1:T(2,128)S(1)}, u32[]{:S(2)}, u32[]{:S(2)}) async-start(f32[2,512,256]{2,0,1:T(2,128)} %copy.144), calls=%async_computation.12 | async-start | bytes 2097152 | tf_op jit(solution)/shard_map/all_to_all | solution.py:64
  464.6 32.5 %all-to-all-start.13 = ((f32[2,512,256]{2,0,1:T(2,128)}), f32[2,512,256]{2,0,1:T(2,128)S(1)}, u32[]{:S(2)}, u32[]{:S(2)}) async-start(f32[2,512,256]{2,0,1:T(2,128)} %copy.147), calls=%async_computation.13 | async-start | bytes 2097152 | tf_op jit(solution)/shard_map/all_to_all | solution.py:65
  497.2 1.0 copy-start
  498.2 33.1 %all-to-all-start.6 = ((f32[2,512,256]{2,0,1:T(2,128)}), f32[2,512,256]{2,0,1:T(2,128)S(1)}, u32[]{:S(2)}, u32[]{:S(2)}) async-start(f32[2,512,256]{2,0,1:T(2,128)} %copy.127), calls=%async_computation.6 | async-start | bytes 2097152 | tf_op jit(solution)/shard_map/all_to_all | solution.py:64
  531.3 33.3 %all-to-all-start.7 = ((f32[2,512,256]{2,0,1:T(2,128)}), f32[2,512,256]{2,0,1:T(2,128)S(1)}, u32[]{:S(2)}, u32[]{:S(2)}) async-start(f32[2,512,256]{2,0,1:T(2,128)} %copy.130), calls=%async_computation.7 | async-start | bytes 2097152 | tf_op jit(solution)/shard_map/all_to_all | solution.py:65
  538.5 3.0 copy-start.1
  543.4 3.0 copy-start.2
  546.4 1.2 copy-start.3
  564.6 22.6 %all-to-all-start.14 = ((f32[32,16,256]{2,1,0:T(8,128)}), f32[32,16,256]{2,1,0:T(8,128)}, u32[]{:S(2)}, u32[]{:S(2)}) async-start(f32[32,16,256]{2,1,0:T(8,128)} %copy.150), calls=%async_computation.14 | async-start | bytes 1048576 | tf_op jit(solution)/shard_map/all_to_all | solution.py:74
  587.2 102.0 %copy-start.9 = (f32[512,256]{1,0:T(8,128)S(1)}, f32[512,256]{1,0:T(8,128)}, u32[]{:S(2)}) copy-start(f32[512,256]{1,0:T(8,128)} %param.7) | copy-start | bytes 1572868
  587.2 104.2 %all-to-all-start.8 = ((f32[32,16,256]{2,1,0:T(8,128)}), f32[32,16,256]{2,1,0:T(8,128)S(1)}, u32[]{:S(2)}, u32[]{:S(2)}) async-start(f32[32,16,256]{2,1,0:T(8,128)} %copy.133), calls=%async_computation.8 | async-start | bytes 1048576 | tf_op jit(solution)/shard_map/all_to_all | solution.py:74
  592.3 96.9 %copy-start.7 = (f32[512,256]{1,0:T(8,128)S(1)}, f32[512,256]{1,0:T(8,128)}, u32[]{:S(2)}) copy-start(f32[512,256]{1,0:T(8,128)} %param.6) | copy-start | bytes 1572868
  592.3 95.2 %all-reduce.2.cloned.1.call-start = ((), (), s32[]{:S(2)}) async-start(), calls=%async_computation.18 | async-start | bytes 524288 | tf_op jit(solution)/shard_map/psum | solution.py:121
  689.2 2.2 copy-start.11
Sparse Core Ops, SparseCore 0:
  596.3 91.1 all-reduce.1
where the time goes:
time: 710 us; the launch traced here: 699 us
  waiting for transfers between devices  345 us (49%)
  matrix products  177 us (25%)
  starting transfers between devices  112 us (16%)
  local copies, waits for them, and re-layouts  43.1 us (6%)
  between operations  15.1 us (2%)
    dot_general x36, matrix products, product_hi(): return jnp.einsum(form, left, right, precision=lax.Precision.HIGHEST)  177 us
    psum x1, waiting for transfers between devices, local(): grad_filter = lax.psum(corr, 'chan') * scale  94.4 us
    all_to_all x3, waiting for transfers between devices, forward_transform(): lax.all_to_all(turned_real, 'seq', split_axis=0, concat_axis=1, tiled=True)  62.5 us
    all_to_all x3, waiting for transfers between devices, inverse_transform(): lax.all_to_all(turned_real, 'seq', split_axis=1, concat_axis=0, tiled=True)  53.5 us
    all_to_all x3, waiting for transfers between devices, forward_transform(): lax.all_to_all(turned_imag, 'seq', split_axis=0, concat_axis=1, tiled=True)  42.3 us
    all_to_all x3, waiting for transfers between devices, inverse_transform(): lax.all_to_all(turned_imag, 'seq', split_axis=1, concat_axis=0, tiled=True)  41 us
    all_to_all x3, waiting for transfers between devices, forward_transform(): lax.all_to_all(block[None], 'seq', split_axis=1, concat_axis=0, tiled=True)  39.9 us
    all_to_all x3, starting transfers between devices, inverse_transform(): lax.all_to_all(turned_real, 'seq', split_axis=1, concat_axis=0, tiled=True)  22 us
  transfers between devices with their start and end apart: 19, of which 14 were waited for; matrix products, arithmetic and copies ran while one was open for 22% of the time, Pallas kernels for 0%

commit v1 on v0

--- a/solution.py
+++ b/solution.py
@@ -118,7 +118,7 @@
     conv = inverse(conv_real, conv_imag)
     grad_gated = inverse(back_real, back_imag)
     corr = inverse(filter_real, filter_imag)
-    grad_filter = lax.psum(corr, "chan") * scale
+    grad_filter = jax.lax.all_gather(corr, "chan").sum(axis=0) * scale
     grad_q = grad_out * conv
     grad_k = grad_gated * values
     grad_v = grad_gated * k_gate

time: 710 us -> 631 us (0.89)
  waiting for transfers between devices: 345 us -> 263 us
    psum x1 -> x0, waiting for transfers between devices: 94.4 us -> none  [local(): grad_filter = lax.psum(corr, 'chan') * scale]
    all_to_all x3, waiting for transfers between devices: 11.2 us -> 26.1 us  [inverse_transform(): lax.all_to_all(spatial, 'seq', split_axis=0, concat_axis=1, tiled=True)]
  transfers between devices with their start and end apart: 19 -> 19, of which waited for: 14 -> 14; matrix products, arithmetic and copies ran while one was open for 22% -> 25% of each run, Pallas kernels for 0% -> 0%
where the time goes in v1:
time: 631 us; the launch traced here: 619 us
  waiting for transfers between devices  263 us (42%)
  matrix products  178 us (28%)
  starting transfers between devices  111 us (18%)
  local copies, waits for them, and re-layouts  42.8 us (7%)
  between operations  15.1 us (2%)
  other arithmetic  8.91 us (1%)
    dot_general x36, matrix products, product_hi(): return jnp.einsum(form, left, right, precision=lax.Precision.HIGHEST)  178 us
    all_to_all x3, waiting for transfers between devices, forward_transform(): lax.all_to_all(turned_real, 'seq', split_axis=0, concat_axis=1, tiled=True)  61.7 us
    all_to_all x3, waiting for transfers between devices, inverse_transform(): lax.all_to_all(turned_real, 'seq', split_axis=1, concat_axis=0, tiled=True)  53.5 us
    all_to_all x3, waiting for transfers between devices, forward_transform(): lax.all_to_all(turned_imag, 'seq', split_axis=0, concat_axis=1, tiled=True)  42.3 us
    all_to_all x3, waiting for transfers between devices, inverse_transform(): lax.all_to_all(turned_imag, 'seq', split_axis=1, concat_axis=0, tiled=True)  40.5 us
    all_to_all x3, waiting for transfers between devices, forward_transform(): lax.all_to_all(block[None], 'seq', split_axis=1, concat_axis=0, tiled=True)  38.7 us
    all_to_all x3, waiting for transfers between devices, inverse_transform(): lax.all_to_all(spatial, 'seq', split_axis=0, concat_axis=1, tiled=True)  26.1 us
    all_to_all x3, starting transfers between devices, inverse_transform(): lax.all_to_all(turned_real, 'seq', split_axis=1, concat_axis=0, tiled=True)  21.3 us
  transfers between devices with their start and end apart: 19, of which 14 were waited for; matrix products, arithmetic and copies ran while one was open for 25% of the time, Pallas kernels for 0%

profile of v1, /device:TPU:32, one launch (start us, length us, event | category | flops | bytes accessed | tf_op | source)
XLA Modules:
  0.0 618.9 jit_solution(6255386853611010709)
XLA Ops:
  8.8 9.8 %all-to-all-start = ((f32[1,512,128]{2,0,1:T(1,128)}), f32[1,512,128]{2,0,1:T(1,128)S(1)}, u32[]{:S(2)}, u32[]{:S(2)}) async-start(f32[1,512,128]{2,0,1:T(1,128)} %bitcast.2), calls=%async_computation | async-start | bytes 524288 | tf_op jit(solution)/shard_map/all_to_all | solution.py:23
  21.1 9.0 %all-to-all-done = f32[1,512,128]{2,0,1:T(1,128)S(1)} async-done(((f32[1,512,128]{2,0,1:T(1,128)}), f32[1,512,128]{2,0,1:T(1,128)S(1)}, u32[]{:S(2)}, u32[]{:S(2)}) %all-to-all-start) | async-done | bytes 262176 | tf_op jit(solution)/shard_map/all_to_all | solution.py:23
  30.1 4.7 all-to-all-start.3
  36.1 15.6 %all-to-all-done.3 = f32[1,512,256]{2,0,1:T(1,128)S(1)} async-done(((f32[1,512,256]{2,0,1:T(1,128)}), f32[1,512,256]{2,0,1:T(1,128)S(1)}, u32[]{:S(2)}, u32[]{:S(2)}) %all-to-all-start.3) | async-done | bytes 524320 | tf_op jit(solution)/shard_map/all_to_all | solution.py:23
  51.7 5.0 all-to-all-start.9
  59.5 14.1 %all-to-all-done.9 = f32[1,512,256]{2,0,1:T(1,128)S(1)} async-done(((f32[1,512,256]{2,0,1:T(1,128)}), f32[1,512,256]{2,0,1:T(1,128)S(1)}, u32[]{:S(2)}, u32[]{:S(2)}) %all-to-all-start.9) | async-done | bytes 524320 | tf_op jit(solution)/shard_map/all_to_all | solution.py:23
  73.6 5.0 all-to-all-start.2
  79.7 15.7 %all-to-all-done.2 = f32[64,16,128]{2,1,0:T(8,128)S(1)} async-done(((f32[64,16,128]{2,1,0:T(8,128)}), f32[64,16,128]{2,1,0:T(8,128)S(1)}, u32[]{:S(2)}, u32[]{:S(2)}) %all-to-all-start.2) | async-done | bytes 524320 | tf_op jit(solution)/shard_map/all_to_all | solution.py:35
  95.5 5.7 all-to-all-start.1
  108.4 9.6 %all-to-all-done.1 = f32[64,16,128]{2,1,0:T(8,128)} async-done(((f32[64,16,128]{2,1,0:T(8,128)}), f32[64,16,128]{2,1,0:T(8,128)}, u32[]{:S(2)}, u32[]{:S(2)}) %all-to-all-start.1) | async-done | bytes 524320 | tf_op jit(solution)/shard_map/all_to_all | solution.py:34
  118.1 5.9 all-to-all-start.10
  125.6 26.6 %all-to-all-done.10 = f32[64,16,256]{2,1,0:T(8,128)} async-done(((f32[64,16,256]{2,1,0:T(8,128)}), f32[64,16,256]{2,1,0:T(8,128)}, u32[]{:S(2)}, u32[]{:S(2)}) %all-to-all-start.10) | async-done | bytes 1048608 | tf_op jit(solution)/shard_map/all_to_all | solution.py:34
  152.1 5.0 all-to-all-start.11
  158.8 26.5 %all-to-all-done.11 = f32[64,16,256]{2,1,0:T(8,128)S(1)} async-done(((f32[64,16,256]{2,1,0:T(8,128)}), f32[64,16,256]{2,1,0:T(8,128)S(1)}, u32[]{:S(2)}, u32[]{:S(2)}) %all-to-all-start.11) | async-done | bytes 1048608 | tf_op jit(solution)/shard_map/all_to_all | solution.py:35
  185.3 5.0 all-to-all-start.4
  192.9 25.5 %all-to-all-done.4 = f32[64,16,256]{2,1,0:T(8,128)S(1)} async-done(((f32[64,16,256]{2,1,0:T(8,128)}), f32[64,16,256]{2,1,0:T(8,128)S(1)}, u32[]{:S(2)}, u32[]{:S(2)}) %all-to-all-start.4) | async-done | bytes 1048608 | tf_op jit(solution)/shard_map/all_to_all | solution.py:34
  218.4 5.0 all-to-all-start.5
  223.4 6.6 %fusion.46 = f32[2,128,512]{2,1,0:T(8,128)S(1)} fusion(f32[2,512,128]{2,1,0:T(8,128)} %bitcast.261), kind=kOutput, calls=%fused_computation.75 | convolution fusion | flops 808976384 | bytes 1048576 | tf_op jit(solution)/shard_map/kn,tnw->tkw/dot_general | solution.py:9
  231.1 5.8 fusion.50
  237.0 6.4 %fusion.4 = f32[2,512,128]{1,2,0:T(8,128)} fusion(f32[2,128,512]{2,1,0:T(8,128)S(1)} %fusion.46, f32[2,512,128]{2,1,0:T(8,128)S(1)} %bitcast.264), kind=kOutput, calls=%fused_computation.28 | convolution fusion | flops 809107456 | bytes 1572864 | tf_op jit(solution)/shard_map/kn,tnw->tkw/dot_general | solution.py:9
  243.4 6.8 %fusion.5 = f32[2,512,128]{1,2,0:T(8,128)} fusion(f32[2,128,512]{2,1,0:T(8,128)S(1)} %fusion.50, f32[2,512,128]{2,1,0:T(8,128)S(1)} %bitcast.262), kind=kOutput, calls=%fused_computation.30 | convolution fusion | flops 809107456 | bytes 1572864 | tf_op jit(solution)/shard_map/kn,tnw->tkw/dot_general | solution.py:9
  252.5 7.5 %fusion.38 = f32[2,256,512]{2,1,0:T(8,128)S(1)} fusion(f32[2,512,256]{2,1,0:T(8,128)S(1)} %bitcast.254), kind=kOutput, calls=%fused_computation.67 | convolution fusion | flops 1614282752 | bytes 2097152 | tf_op jit(solution)/shard_map/kn,tnw->tkw/dot_general | solution.py:9
  260.0 8.0 %fusion.48 = f32[2,256,512]{2,1,0:T(8,128)} fusion(f32[2,512,256]{2,1,0:T(8,128)S(1)} %bitcast.236), kind=kOutput, calls=%fused_computation.77 | convolution fusion | flops 1614282752 | bytes 2097152 | tf_op jit(solution)/shard_map/kn,tnw->tkw/dot_general | solution.py:9
  268.0 8.1 %fusion.36 = f32[2,256,512]{2,1,0:T(8,128)} fusion(f32[2,512,256]{2,1,0:T(8,128)S(1)} %bitcast.256), kind=kOutput, calls=%fused_computation.65 | convolution fusion | flops 1614282752 | bytes 2097152 | tf_op jit(solution)/shard_map/kn,tnw->tkw/dot_general | solution.py:9
  276.1 8.0 %fusion.1 = f32[2,512,256]{1,2,0:T(8,128)} fusion(f32[2,256,512]{2,1,0:T(8,128)S(1)} %fusion.38, f32[2,512,256]{2,1,0:T(8,128)S(1)} %bitcast.257), kind=kOutput, calls=%fused_computation.18 | convolution fusion | flops 1614544896 | bytes 3145728 | tf_op jit(solution)/shard_map/kn,tnw->tkw/dot_general | solution.py:9
  284.2 7.5 %fusion.44 = f32[2,256,512]{2,1,0:T(8,128)S(1)} fusion(f32[2,512,256]{2,1,0:T(8,128)S(1)} %bitcast.258), kind=kOutput, calls=%fused_computation.73 | convolution fusion | flops 1614282752 | bytes 2097152 | tf_op jit(solution)/shard_map/kn,tnw->tkw/dot_general | solution.py:9
  291.7 7.8 %fusion.3 = f32[2,512,256]{1,2,0:T(8,128)S(1)} fusion(f32[2,256,512]{2,1,0:T(8,128)S(1)} %copy-done.28, f32[2,512,256]{2,1,0:T(8,128)S(1)} %bitcast.259), kind=kOutput, calls=%fused_computation.24 | convolution fusion | flops 1614544896 | bytes 3145728 | tf_op jit(solution)/shard_map/kn,tnw->tkw/dot_general | solution.py:9
  299.6 7.6 %fusion = f32[2,512,256]{1,2,0:T(8,128)S(1)} fusion(f32[2,256,512]{2,1,0:T(8,128)S(1)} %copy-done.26, f32[2,512,256]{2,1,0:T(8,128)S(1)} %bitcast.255), kind=kOutput, calls=%fused_computation.16 | convolution fusion | flops 1614544896 | bytes 3145728 | tf_op jit(solution)/shard_map/kn,tnw->tkw/dot_general | solution.py:9
  307.2 11.9 %multiply_add_fusion = (f32[2,512,256]{1,2,0:T(8,128)S(1)}, f32[2,512,256]{1,2,0:T(8,128)S(1)}, f32[2,512,256]{1,2,0:T(8,128)}, f32[2,512,256]{1,2,0:T(8,128)}, ...) fusion(f32[2,512,256]{1,2,0:T(8,128)S(1)} %fusion, f32[2,512,256]{1,2,0:T(8,128)S(1)} %fusion.3, ...), kind=kOutput, calls=%fused_computation.82 | convolution fusion | flops 1619263488 | bytes 12582912 | tf_op jit(solution)/shard_map/kn,tnw->tkw/dot_general | solution.py:9
  319.2 6.2 fusion.28
  325.5 5.3 fusion.30
  330.8 5.3 convolution_add_fusion.4
  336.2 5.4 add_bitcast_fusion.2
  342.6 8.6 %all-to-all-start.15 = ((f32[2,512,128]{2,0,1:T(2,128)}), f32[2,512,128]{2,0,1:T(2,128)S(1)}, u32[]{:S(2)}, u32[]{:S(2)}) async-start(f32[2,512,128]{2,0,1:T(2,128)} %copy.149), calls=%async_computation.15 | async-start | bytes 1048576 | tf_op jit(solution)/shard_map/all_to_all | solution.py:64
  352.2 6.3 %fusion.32 = f32[2,256,512]{2,1,0:T(8,128)S(1)} fusion(f32[2,512,256]{1,2,0:T(8,128)S(1)} %copy-done.12), kind=kOutput, calls=%fused_computation.61 | convolution fusion | flops 1614282752 | bytes 2097152 | tf_op jit(solution)/shard_map/nk,tkw->tnw/dot_general | solution.py:9
  358.5 6.7 %fusion.34 = f32[2,256,512]{2,1,0:T(8,128)} fusion(f32[2,512,256]{1,2,0:T(8,128)S(1)} %copy-done.14), kind=kOutput, calls=%fused_computation.63 | convolution fusion | flops 1614282752 | bytes 2097152 | tf_op jit(solution)/shard_map/nk,tkw->tnw/dot_general | solution.py:9
  365.3 6.7 %convolution_add_fusion = f32[2,256,512]{2,1,0:T(8,128)} fusion(f32[2,256,512]{2,1,0:T(8,128)S(1)} %fusion.32, f32[2,512,256]{1,2,0:T(8,128)S(1)} %copy-done.14), kind=kOutput, calls=%fused_computation.13 | convolution fusion | flops 1614544896 | bytes 3145728 | tf_op jit(solution)/shard_map/nk,tkw->tnw/dot_general | solution.py:9
  372.0 8.6 %all-to-all-start.16 = ((f32[2,512,128]{2,0,1:T(2,128)}), f32[2,512,128]{2,0,1:T(2,128)S(1)}, u32[]{:S(2)}, u32[]{:S(2)}) async-start(f32[2,512,128]{2,0,1:T(2,128)} %copy.152), calls=%async_computation.16 | async-start | bytes 1048576 | tf_op jit(solution)/shard_map/all_to_all | solution.py:65
  380.6 6.3 %fusion.40 = f32[2,256,512]{2,1,0:T(8,128)S(1)} fusion(f32[2,512,256]{1,2,0:T(8,128)S(1)} %copy-done.4), kind=kOutput, calls=%fused_computation.69 | convolution fusion | flops 1614282752 | bytes 2097152 | tf_op jit(solution)/shard_map/nk,tkw->tnw/dot_general | solution.py:9
  387.0 6.7 %convolution_subtract_fusion = f32[2,256,512]{2,1,0:T(8,128)} fusion(f32[2,256,512]{2,1,0:T(8,128)S(1)} %copy-done.27, f32[2,512,256]{1,2,0:T(8,128)S(1)} %copy-done.13), kind=kOutput, calls=%fused_computation.14 | convolution fusion | flops 1614544896 | bytes 3145728 | tf_op jit(solution)/shard_map/nk,tkw->tnw/dot_general | solution.py:9
  393.7 6.7 %convolution_add_fusion.2 = f32[2,256,512]{2,1,0:T(8,128)} fusion(f32[2,256,512]{2,1,0:T(8,128)S(1)} %fusion.40, f32[2,512,256]{1,2,0:T(8,128)S(1)} %copy-done.11), kind=kOutput, calls=%fused_computation.19 | convolution fusion | flops 1614544896 | bytes 3145728 | tf_op jit(solution)/shard_map/nk,tkw->tnw/dot_general | solution.py:9
  403.1 8.8 %all-to-all-start.17 = ((f32[32,16,128]{2,1,0:T(8,128)}), f32[32,16,128]{2,1,0:T(8,128)S(1)}, u32[]{:S(2)}, u32[]{:S(2)}) async-start(f32[32,16,128]{2,1,0:T(8,128)} %copy.155), calls=%async_computation.17 | async-start | bytes 524288 | tf_op jit(solution)/shard_map/all_to_all | solution.py:74
  411.9 6.3 %fusion.42 = f32[2,256,512]{2,1,0:T(8,128)S(1)} fusion(f32[2,512,256]{1,2,0:T(8,128)S(1)} %copy-done.11), kind=kOutput, calls=%fused_computation.71 | convolution fusion | flops 1614282752 | bytes 2097152 | tf_op jit(solution)/shard_map/nk,tkw->tnw/dot_general | solution.py:9
  418.3 7.2 %add_bitcast_fusion = (f32[2,512,256]{1,2,0:T(8,128)}, f32[2,512,256]{1,2,0:T(8,128)}, f32[2,512,256]{1,2,0:T(8,128)S(1)}, f32[2,512,256]{1,2,0:T(8,128)S(1)}) fusion(f32[2,256,512]{2,1,0:T(8,128)S(1)} %copy-done.20, f32[2,256,512]{2,1,0:T(8,128)S(1)} %copy-done.19, f32[2,512]{1,0:T(2,128)S(1)} %get-tuple-element.33, f32[2,512]{1,0:T(2,128)S(1)} %get-tuple-element.32, ...), kind=kOutput, calls=%fused_computation.83 | convolution fusion | flops 1617690624 | bytes 9445376 | tf_op jit(solution)/shard_map/nk,tkw->tnw/dot_general | solution.py:9
  425.5 2.3 copy.142
  427.8 8.3 %all-to-all-start.12 = ((f32[2,512,256]{2,0,1:T(2,128)}), f32[2,512,256]{2,0,1:T(2,128)S(1)}, u32[]{:S(2)}, u32[]{:S(2)}) async-start(f32[2,512,256]{2,0,1:T(2,128)} %copy.142), calls=%async_computation.12 | async-start | bytes 2097152 | tf_op jit(solution)/shard_map/all_to_all | solution.py:64
  437.4 26.7 %all-to-all-done.12 = f32[2,512,256]{2,0,1:T(2,128)S(1)} async-done(((f32[2,512,256]{2,0,1:T(2,128)}), f32[2,512,256]{2,0,1:T(2,128)S(1)}, u32[]{:S(2)}, u32[]{:S(2)}) %all-to-all-start.12) | async-done | bytes 1048608 | tf_op jit(solution)/shard_map/all_to_all | solution.py:64
  464.1 4.4 all-to-all-start.6
  469.8 26.8 %all-to-all-done.6 = f32[2,512,256]{2,0,1:T(2,128)S(1)} async-done(((f32[2,512,256]{2,0,1:T(2,128)}), f32[2,512,256]{2,0,1:T(2,128)S(1)}, u32[]{:S(2)}, u32[]{:S(2)}) %all-to-all-start.6) | async-done | bytes 1048608 | tf_op jit(solution)/shard_map/all_to_all | solution.py:64
  496.6 5.0 all-to-all-start.7
  501.7 2.3 copy.145
  503.9 25.9 %all-to-all-done.7 = f32[2,512,256]{2,0,1:T(2,128)S(1)} async-done(((f32[2,512,256]{2,0,1:T(2,128)}), f32[2,512,256]{2,0,1:T(2,128)S(1)}, u32[]{:S(2)}, u32[]{:S(2)}) %all-to-all-start.7) | async-done | bytes 1048608 | tf_op jit(solution)/shard_map/all_to_all | solution.py:65
  530.8 5.0 all-to-all-start.13
  536.6 1.8 copy.127
  538.4 2.9 all_to_all.229
  541.5 1.8 copy.130
  543.3 3.0 all_to_all.233
  549.3 14.7 %all-to-all-done.13 = f32[2,512,256]{2,0,1:T(2,128)S(1)} async-done(((f32[2,512,256]{2,0,1:T(2,128)}), f32[2,512,256]{2,0,1:T(2,128)S(1)}, u32[]{:S(2)}, u32[]{:S(2)}) %all-to-all-start.13) | async-done | bytes 1048608 | tf_op jit(solution)/shard_map/all_to_all | solution.py:65
  563.9 5.6 all-to-all-start.8
  575.4 11.1 %all-to-all-done.8 = f32[32,16,256]{2,1,0:T(8,128)} async-done(((f32[32,16,256]{2,1,0:T(8,128)}), f32[32,16,256]{2,1,0:T(8,128)}, u32[]{:S(2)}, u32[]{:S(2)}) %all-to-all-start.8) | async-done | bytes 524320 | tf_op jit(solution)/shard_map/all_to_all | solution.py:74
  586.5 5.0 all-to-all-start.14
  591.5 1.9 bitcast_multiply_fusion.10
  593.4 15.0 %all-to-all-done.14 = f32[32,16,256]{2,1,0:T(8,128)S(1)} async-done(((f32[32,16,256]{2,1,0:T(8,128)}), f32[32,16,256]{2,1,0:T(8,128)S(1)}, u32[]{:S(2)}, u32[]{:S(2)}) %all-to-all-start.14) | async-done | bytes 524320 | tf_op jit(solution)/shard_map/all_to_all | solution.py:74
  609.5 1.7 reduce_sum.29
  (125 shorter events, 45.7 us)
Async XLA Ops:
  8.8 26.0 %copy-start.5 = (f32[512,256]{1,0:T(8,128)S(1)}, f32[512,256]{1,0:T(8,128)}, u32[]{:S(2)}) copy-start(f32[512,256]{1,0:T(8,128)} %param.9) | copy-start | bytes 1572868
  8.8 26.0 %copy-start.22 = (f32[512,256]{1,0:T(8,128)S(1)}, f32[512,256]{1,0:T(8,128)}, u32[]{:S(2)}) copy-start(f32[512,256]{1,0:T(8,128)} %param.5) | copy-start | bytes 1572868
  8.8 21.2 %all-to-all-start = ((f32[1,512,128]{2,0,1:T(1,128)}), f32[1,512,128]{2,0,1:T(1,128)S(1)}, u32[]{:S(2)}, u32[]{:S(2)}) async-start(f32[1,512,128]{2,0,1:T(1,128)} %bitcast.2), calls=%async_computation | async-start | bytes 524288 | tf_op jit(solution)/shard_map/all_to_all | solution.py:23
  30.1 21.6 %all-to-all-start.3 = ((f32[1,512,256]{2,0,1:T(1,128)}), f32[1,512,256]{2,0,1:T(1,128)S(1)}, u32[]{:S(2)}, u32[]{:S(2)}) async-start(f32[1,512,256]{2,0,1:T(1,128)} %broadcast_in_dim.7), calls=%async_computation.3 | async-start | bytes 1048576 | tf_op jit(solution)/shard_map/all_to_all | solution.py:23
  51.7 21.9 %all-to-all-start.9 = ((f32[1,512,256]{2,0,1:T(1,128)}), f32[1,512,256]{2,0,1:T(1,128)S(1)}, u32[]{:S(2)}, u32[]{:S(2)}) async-start(f32[1,512,256]{2,0,1:T(1,128)} %broadcast_in_dim.8), calls=%async_computation.9 | async-start | bytes 1048576 | tf_op jit(solution)/shard_map/all_to_all | solution.py:23
  73.6 21.9 %all-to-all-start.2 = ((f32[64,16,128]{2,1,0:T(8,128)}), f32[64,16,128]{2,1,0:T(8,128)S(1)}, u32[]{:S(2)}, u32[]{:S(2)}) async-start(f32[64,16,128]{2,1,0:T(8,128)} %copy.110), calls=%async_computation.2 | async-start | bytes 1048576 | tf_op jit(solution)/shard_map/all_to_all | solution.py:35
  95.5 8.3 %copy-start.9 = (f32[64,16,128]{2,1,0:T(8,128)}, f32[64,16,128]{2,1,0:T(8,128)S(1)}, u32[]{:S(2)}) copy-start(f32[64,16,128]{2,1,0:T(8,128)S(1)} %all-to-all-done.2) | copy-start | bytes 1572868
  95.5 22.6 %all-to-all-start.1 = ((f32[64,16,128]{2,1,0:T(8,128)}), f32[64,16,128]{2,1,0:T(8,128)}, u32[]{:S(2)}, u32[]{:S(2)}) async-start(f32[64,16,128]{2,1,0:T(8,128)} %copy.107), calls=%async_computation.1 | async-start | bytes 1048576 | tf_op jit(solution)/shard_map/all_to_all | solution.py:34
  118.1 34.1 %all-to-all-start.10 = ((f32[64,16,256]{2,1,0:T(8,128)}), f32[64,16,256]{2,1,0:T(8,128)}, u32[]{:S(2)}, u32[]{:S(2)}) async-start(f32[64,16,256]{2,1,0:T(8,128)} %copy.134), calls=%async_computation.10 | async-start | bytes 2097152 | tf_op jit(solution)/shard_map/all_to_all | solution.py:34
  152.1 33.1 %all-to-all-start.11 = ((f32[64,16,256]{2,1,0:T(8,128)}), f32[64,16,256]{2,1,0:T(8,128)S(1)}, u32[]{:S(2)}, u32[]{:S(2)}) async-start(f32[64,16,256]{2,1,0:T(8,128)} %copy.137), calls=%async_computation.11 | async-start | bytes 2097152 | tf_op jit(solution)/shard_map/all_to_all | solution.py:35
  185.3 33.1 %all-to-all-start.4 = ((f32[64,16,256]{2,1,0:T(8,128)}), f32[64,16,256]{2,1,0:T(8,128)S(1)}, u32[]{:S(2)}, u32[]{:S(2)}) async-start(f32[64,16,256]{2,1,0:T(8,128)} %copy.115), calls=%async_computation.4 | async-start | bytes 2097152 | tf_op jit(solution)/shard_map/all_to_all | solution.py:34
  190.3 1.8 copy-start.10
  218.4 65.7 %all-to-all-start.5 = ((f32[64,16,256]{2,1,0:T(8,128)}), f32[64,16,256]{2,1,0:T(8,128)S(1)}, u32[]{:S(2)}, u32[]{:S(2)}) async-start(f32[64,16,256]{2,1,0:T(8,128)} %copy.118), calls=%async_computation.5 | async-start | bytes 2097152 | tf_op jit(solution)/shard_map/all_to_all | solution.py:35
  237.0 6.4 %copy-start.25 = (f32[2,32,16,128]{3,2,1,0:T(8,128)S(1)}, f32[2,32,16,128]{3,2,1,0:T(8,128)}, u32[]{:S(2)}) copy-start(f32[2,32,16,128]{3,2,1,0:T(8,128)} %copy.111) | copy-start | bytes 1572868
  251.5 1.0 copy-start.16
  284.2 7.5 %copy-start.28 = (f32[2,256,512]{2,1,0:T(8,128)S(1)}, f32[2,256,512]{2,1,0:T(8,128)}, u32[]{:S(2)}) copy-start(f32[2,256,512]{2,1,0:T(8,128)} %fusion.48) | copy-start | bytes 3145732
  291.7 7.8 %copy-start.17 = (f32[2,32,16,256]{3,2,1,0:T(8,128)S(1)}, f32[2,32,16,256]{3,2,1,0:T(8,128)}, u32[]{:S(2)}) copy-start(f32[2,32,16,256]{3,2,1,0:T(8,128)} %copy-done.16) | copy-start | bytes 3145732
  291.7 7.8 %copy-start.26 = (f32[2,256,512]{2,1,0:T(8,128)S(1)}, f32[2,256,512]{2,1,0:T(8,128)}, u32[]{:S(2)}) copy-start(f32[2,256,512]{2,1,0:T(8,128)} %fusion.36) | copy-start | bytes 3145732
  299.6 7.6 %copy-start.15 = (f32[2,512,256]{1,2,0:T(8,128)S(1)}, f32[2,512,256]{1,2,0:T(8,128)}, u32[]{:S(2)}) copy-start(f32[2,512,256]{1,2,0:T(8,128)} %fusion.1) | copy-start | bytes 3145732
  299.6 7.6 %copy-start.23 = (f32[2,512,128]{1,2,0:T(8,128)S(1)}, f32[2,512,128]{1,2,0:T(8,128)}, u32[]{:S(2)}) copy-start(f32[2,512,128]{1,2,0:T(8,128)} %fusion.4) | copy-start | bytes 1572868
  299.6 7.6 %copy-start.24 = (f32[2,512,128]{1,2,0:T(8,128)S(1)}, f32[2,512,128]{1,2,0:T(8,128)}, u32[]{:S(2)}) copy-start(f32[2,512,128]{1,2,0:T(8,128)} %fusion.5) | copy-start | bytes 1572868
  325.5 5.3 copy-start.29
  341.6 10.6 %copy-start.12 = (f32[2,512,256]{1,2,0:T(8,128)S(1)}, f32[2,512,256]{1,2,0:T(8,128)}, u32[]{:S(2)}) copy-start(f32[2,512,256]{1,2,0:T(8,128)} %get-tuple-element.18) | copy-start | bytes 3145732
  342.6 29.4 %all-to-all-start.15 = ((f32[2,512,128]{2,0,1:T(2,128)}), f32[2,512,128]{2,0,1:T(2,128)S(1)}, u32[]{:S(2)}, u32[]{:S(2)}) async-start(f32[2,512,128]{2,0,1:T(2,128)} %copy.149), calls=%async_computation.15 | async-start | bytes 1048576 | tf_op jit(solution)/shard_map/all_to_all | solution.py:64
  352.2 6.3 %copy-start.14 = (f32[2,512,256]{1,2,0:T(8,128)S(1)}, f32[2,512,256]{1,2,0:T(8,128)}, u32[]{:S(2)}) copy-start(f32[2,512,256]{1,2,0:T(8,128)} %get-tuple-element.19) | copy-start | bytes 3145732
  365.3 15.3 %copy-start.4 = (f32[2,512,256]{1,2,0:T(8,128)S(1)}, f32[2,512,256]{1,2,0:T(8,128)}, u32[]{:S(2)}) copy-start(f32[2,512,256]{1,2,0:T(8,128)} %get-tuple-element.20) | copy-start | bytes 3145732
  372.0 29.3 %all-to-all-start.16 = ((f32[2,512,128]{2,0,1:T(2,128)}), f32[2,512,128]{2,0,1:T(2,128)S(1)}, u32[]{:S(2)}, u32[]{:S(2)}) async-start(f32[2,512,128]{2,0,1:T(2,128)} %copy.152), calls=%async_computation.16 | async-start | bytes 1048576 | tf_op jit(solution)/shard_map/all_to_all | solution.py:65
  380.6 6.4 %copy-start.13 = (f32[2,512,256]{1,2,0:T(8,128)S(1)}, f32[2,512,256]{1,2,0:T(8,128)}, u32[]{:S(2)}) copy-start(f32[2,512,256]{1,2,0:T(8,128)} %get-tuple-element.18) | copy-start | bytes 3145732
  380.6 6.4 %copy-start.27 = (f32[2,256,512]{2,1,0:T(8,128)S(1)}, f32[2,256,512]{2,1,0:T(8,128)}, u32[]{:S(2)}) copy-start(f32[2,256,512]{2,1,0:T(8,128)} %fusion.34) | copy-start | bytes 3145732
  387.0 6.7 %copy-start.11 = (f32[2,512,256]{1,2,0:T(8,128)S(1)}, f32[2,512,256]{1,2,0:T(8,128)}, u32[]{:S(2)}) copy-start(f32[2,512,256]{1,2,0:T(8,128)} %get-tuple-element.21) | copy-start | bytes 3145732
  403.1 24.7 %all-to-all-start.17 = ((f32[32,16,128]{2,1,0:T(8,128)}), f32[32,16,128]{2,1,0:T(8,128)S(1)}, u32[]{:S(2)}, u32[]{:S(2)}) async-start(f32[32,16,128]{2,1,0:T(8,128)} %copy.155), calls=%async_computation.17 | async-start | bytes 524288 | tf_op jit(solution)/shard_map/all_to_all | solution.py:74
  411.9 6.4 %copy-start.19 = (f32[2,256,512]{2,1,0:T(8,128)S(1)}, f32[2,256,512]{2,1,0:T(8,128)}, u32[]{:S(2)}) copy-start(f32[2,256,512]{2,1,0:T(8,128)} %convolution_add_fusion) | copy-start | bytes 3145732
  411.9 6.4 %copy-start.20 = (f32[2,256,512]{2,1,0:T(8,128)S(1)}, f32[2,256,512]{2,1,0:T(8,128)}, u32[]{:S(2)}) copy-start(f32[2,256,512]{2,1,0:T(8,128)} %convolution_subtract_fusion) | copy-start | bytes 3145732
  411.9 6.4 %copy-start.21 = (f32[2,256,512]{2,1,0:T(8,128)S(1)}, f32[2,256,512]{2,1,0:T(8,128)}, u32[]{:S(2)}) copy-start(f32[2,256,512]{2,1,0:T(8,128)} %convolution_add_fusion.2) | copy-start | bytes 3145732
  427.8 9.6 %copy-start.18 = (f32[32,16,128]{2,1,0:T(8,128)}, f32[32,16,128]{2,1,0:T(8,128)S(1)}, u32[]{:S(2)}) copy-start(f32[32,16,128]{2,1,0:T(8,128)S(1)} %all-to-all-done.17) | copy-start | bytes 786436
  427.8 36.3 %all-to-all-start.12 = ((f32[2,512,256]{2,0,1:T(2,128)}), f32[2,512,256]{2,0,1:T(2,128)S(1)}, u32[]{:S(2)}, u32[]{:S(2)}) async-start(f32[2,512,256]{2,0,1:T(2,128)} %copy.142), calls=%async_computation.12 | async-start | bytes 2097152 | tf_op jit(solution)/shard_map/all_to_all | solution.py:64
  464.1 32.5 %all-to-all-start.6 = ((f32[2,512,256]{2,0,1:T(2,128)}), f32[2,512,256]{2,0,1:T(2,128)S(1)}, u32[]{:S(2)}, u32[]{:S(2)}) async-start(f32[2,512,256]{2,0,1:T(2,128)} %copy.125), calls=%async_computation.6 | async-start | bytes 2097152 | tf_op jit(solution)/shard_map/all_to_all | solution.py:64
  496.6 33.1 %all-to-all-start.7 = ((f32[2,512,256]{2,0,1:T(2,128)}), f32[2,512,256]{2,0,1:T(2,128)S(1)}, u32[]{:S(2)}, u32[]{:S(2)}) async-start(f32[2,512,256]{2,0,1:T(2,128)} %copy.128), calls=%async_computation.7 | async-start | bytes 2097152 | tf_op jit(solution)/shard_map/all_to_all | solution.py:65
  529.8 1.0 copy-start
  530.8 33.1 %all-to-all-start.13 = ((f32[2,512,256]{2,0,1:T(2,128)}), f32[2,512,256]{2,0,1:T(2,128)S(1)}, u32[]{:S(2)}, u32[]{:S(2)}) async-start(f32[2,512,256]{2,0,1:T(2,128)} %copy.145), calls=%async_computation.13 | async-start | bytes 2097152 | tf_op jit(solution)/shard_map/all_to_all | solution.py:65
  535.8 73.6 %all-gather.2.cloned.1.call-start = ((), (), s32[]{:S(2)}) async-start(), calls=%async_computation.18 | async-start | bytes 2359296 | tf_op jit(solution)/shard_map/all_gather | solution.py:121
  536.6 4.7 copy-start.1
  541.5 4.8 copy-start.2
  546.2 1.2 copy-start.3
  563.9 22.6 %all-to-all-start.8 = ((f32[32,16,256]{2,1,0:T(8,128)}), f32[32,16,256]{2,1,0:T(8,128)}, u32[]{:S(2)}, u32[]{:S(2)}) async-start(f32[32,16,256]{2,1,0:T(8,128)} %copy.131), calls=%async_computation.8 | async-start | bytes 1048576 | tf_op jit(solution)/shard_map/all_to_all | solution.py:74
  573.5 18.0 %copy-start.6 = (f32[512,256]{1,0:T(8,128)S(1)}, f32[512,256]{1,0:T(8,128)}, u32[]{:S(2)}) copy-start(f32[512,256]{1,0:T(8,128)} %param.9) | copy-start | bytes 1572868
  574.2 34.1 %copy-start.7 = (f32[512,256]{1,0:T(8,128)S(1)}, f32[512,256]{1,0:T(8,128)}, u32[]{:S(2)}) copy-start(f32[512,256]{1,0:T(8,128)} %param.6) | copy-start | bytes 1572868
  574.3 34.1 %copy-start.8 = (f32[512,256]{1,0:T(8,128)S(1)}, f32[512,256]{1,0:T(8,128)}, u32[]{:S(2)}) copy-start(f32[512,256]{1,0:T(8,128)} %param.7) | copy-start | bytes 1572868
  586.5 21.9 %all-to-all-start.14 = ((f32[32,16,256]{2,1,0:T(8,128)}), f32[32,16,256]{2,1,0:T(8,128)S(1)}, u32[]{:S(2)}, u32[]{:S(2)}) async-start(f32[32,16,256]{2,1,0:T(8,128)} %copy.148), calls=%async_computation.14 | async-start | bytes 1048576 | tf_op jit(solution)/shard_map/all_to_all | solution.py:74
Sparse Core Ops, SparseCore 0:
  539.8 62.7 all-gather.1
